TPU v7x, 128 devices: a whole 4x4x4 slice. The times are simulated.
128 devices in a mesh: cfg: 2 (over y_hi), group: 16 (over y_lo, x, core), mp: 4 (over z).
Axes of the slice: x: 4, y: 4 (y_hi: 2, y_lo: 2; y = y_hi * 2 + y_lo), z: 4, core: 2. Of those that a mesh axis runs over, the one named last changes fastest.
Arguments:
- latents: float32 [16384, 64], P(('group', 'mp')), may hold values from -0.6 to 0.6
- text_hidden: bfloat16 [2, 8192, 3072], P('cfg', ('group', 'mp')), may hold values from -6 to 6
- w_img_in: bfloat16 [64, 3072], replicated, may hold values from -0.75 to 0.75
- w_img_qkv: bfloat16 [3072, 4608], P(None, 'mp'), may hold values from -1 to 1
- w_txt_kv: bfloat16 [3072, 3072], P(None, 'mp'), may hold values from -0.109375 to 0.109375
- q_gain: float32 [128], replicated, may hold values from 0.25 to 1.75
- k_gain: float32 [128], replicated, may hold values from 0.25 to 1.75
- w_out: bfloat16 [1536, 3072], replicated, may hold values from -1 to 1
- w_final: bfloat16 [3072, 64], replicated, may hold values from -0.109375 to 0.109375
- mod_img: float32 [8, 3, 3072], replicated, may hold values from -3 to 3
- mod_txt: float32 [8, 2, 3072], replicated, may hold values from -3 to 3
- mod_final: float32 [8, 2, 3072], replicated, may hold values from -3 to 3
- guide: float32 [16], replicated, may hold values from 1.5 to 5
- step_size: float32 [8], replicated, may hold values from 0.02 to 0.3
- img_len: int32 [16], replicated, may hold values from 1 to 1024, as said below
- txt_len: int32 [16], replicated, may hold values from 1 to 512, as said below
- split_flag: int32 [2, 16], replicated, may hold values from 0 to 1, as said below
- tstep: int32 [16], replicated, may hold values from 0 to 7
Outputs:
- velocity: float32 [2, 8192, 64], P('cfg', ('group', 'mp'))
- next_latents: float32 [2, 8192, 64], P('cfg', ('group', 'mp'))
Inputs may be any that keep to these rules, and one draw needn't show every extreme that they name: `img_len`: some group has exactly 1024 live image tokens. `txt_len`: some group has exactly 512 live text tokens. `split_flag`: entries [c, 2j] and [c, 2j + 1] are equal; at least one such pair carries 1 and at least one carries 0.
All inputs are finite; a program needn't handle non-finite values.
Results may differ from a plain program's by a relative error of at most 0.035.
Values may be sent and summed in bfloat16 or wider, within the bound.
A program may use at most 192 MiB of HBM per device.

v0:
```python
import jax
import jax.numpy as jnp
from jax import lax
from jax.sharding import PartitionSpec as P

HD = 128


def partner(value, axis, bit):
    mask = 2**bit
    pairs = [(source, source ^ mask) for source in range(lax.axis_size(axis))]
    return lax.ppermute(value, axis, pairs)


def layer_norm(values):
    center = values - jnp.mean(values, -1, keepdims=True)
    spread = jnp.mean(center * center, -1, keepdims=True)
    return center * lax.rsqrt(spread + 1e-06)


def head_norm(values, gain):
    return values * lax.rsqrt(jnp.mean(values * values, -1, keepdims=True) + 1e-06) * gain


def pick_entry(table, index):
    return lax.dynamic_index_in_dim(table, index, 0, keepdims=False)


def local(
    latents,
    text_hidden,
    w_img_in,
    w_img_qkv,
    w_txt_kv,
    q_gain,
    k_gain,
    w_out,
    w_final,
    mod_img,
    mod_txt,
    mod_final,
    guide,
    step_size,
    img_len,
    txt_len,
    split_flag,
    tstep,
):
    group_index = lax.axis_index("group")
    mp_index = lax.axis_index("mp")
    cfg_index = lax.axis_index("cfg")
    mp_count = lax.axis_size("mp")
    mate_index = jnp.bitwise_xor(group_index, 1)
    step_index = pick_entry(tstep, group_index)
    mod_rows = pick_entry(mod_img, step_index)
    text_rows = pick_entry(mod_txt, step_index)
    final_rows = pick_entry(mod_final, step_index)
    shard_rows = latents.shape[0]
    half_rows = shard_rows // 2
    full_img = shard_rows * mp_count
    full_txt = text_hidden.shape[1] * mp_count
    local_heads = w_img_qkv.shape[1] // (3 * HD)
    x_img = jnp.dot(latents.astype(jnp.bfloat16), w_img_in, preferred_element_type=jnp.float32)
    img_mod = (layer_norm(x_img) * (1.0 + mod_rows[1]) + mod_rows[0]).astype(jnp.bfloat16)
    txt_mod = (
        layer_norm(text_hidden[0].astype(jnp.float32)) * (1.0 + text_rows[1]) + text_rows[0]
    ).astype(jnp.bfloat16)
    img_full, txt_full = (
        lax.all_gather(img_mod, "mp", axis=0, tiled=True),
        lax.all_gather(txt_mod, "mp", axis=0, tiled=True),
    )
    qkv = jnp.dot(img_full, w_img_qkv, preferred_element_type=jnp.float32).reshape(
        full_img, local_heads, 3, HD
    )
    query = head_norm(qkv[:, :, 0], q_gain).astype(jnp.bfloat16)
    key_img = head_norm(qkv[:, :, 1], k_gain).astype(jnp.bfloat16)
    value_img = qkv[:, :, 2].astype(jnp.bfloat16)
    text_kv = jnp.dot(txt_full, w_txt_kv, preferred_element_type=jnp.float32).reshape(
        full_txt, local_heads, 2, HD
    )
    key_txt = head_norm(text_kv[:, :, 0], k_gain).astype(jnp.bfloat16)
    value_txt = text_kv[:, :, 1].astype(jnp.bfloat16)
    key_rows = jnp.concatenate([key_txt, key_img], axis=0)
    value_rows = jnp.concatenate([value_txt, value_img], axis=0)
    mate_keys, mate_values = partner((key_rows, value_rows), "group", 0)
    spots_txt = jnp.arange(full_txt, dtype=jnp.int32)
    spots_img = jnp.arange(full_img, dtype=jnp.int32)

    def live_rows(index):
        return jnp.concatenate(
            [spots_txt < pick_entry(txt_len, index), spots_img < pick_entry(img_len, index)]
        )

    flagged = pick_entry(pick_entry(split_flag, cfg_index), group_index) == 1
    live = jnp.concatenate([live_rows(group_index), live_rows(mate_index) & flagged])
    all_keys = jnp.concatenate([key_rows, mate_keys], axis=0)
    all_values = jnp.concatenate([value_rows, mate_values], axis=0)
    scores = jnp.einsum(
        "qhe,khe->hqk", query, all_keys, preferred_element_type=jnp.float32
    ) * HD ** (-0.5)
    scores = jnp.where(live[None, None, :], scores, -1e30)
    weights = jnp.exp(scores - jnp.max(scores, -1, keepdims=True))
    probs = (weights / jnp.sum(weights, -1, keepdims=True)).astype(jnp.bfloat16)
    mixed = jnp.einsum(
        "hqk,khe->qhe", probs, all_values, preferred_element_type=jnp.float32
    ).astype(jnp.bfloat16)
    mixed = mixed.reshape(full_img, local_heads * HD)
    w_local = lax.dynamic_slice_in_dim(w_out, mp_index * local_heads * HD, local_heads * HD, 0)
    attended = lax.psum_scatter(
        jnp.dot(mixed, w_local, preferred_element_type=jnp.float32),
        "mp",
        scatter_dimension=0,
        tiled=True,
    )
    hidden = x_img + mod_rows[2] * attended
    final = (layer_norm(hidden) * (1.0 + final_rows[1]) + final_rows[0]).astype(jnp.bfloat16)
    own_velocity = jnp.dot(final, w_final, preferred_element_type=jnp.float32)
    scale = pick_entry(guide, group_index)
    other_velocity = partner(own_velocity.astype(jnp.bfloat16), "cfg", 0).astype(own_velocity.dtype)
    is_cond = cfg_index == 0
    cond_part = jnp.where(is_cond, own_velocity, other_velocity)
    uncond_part = jnp.where(is_cond, other_velocity, own_velocity)
    guided_all = uncond_part + scale * (cond_part - uncond_part)
    guided = lax.dynamic_slice_in_dim(guided_all, cfg_index * half_rows, half_rows, 0)
    row_place = (
        mp_index * shard_rows + cfg_index * half_rows + jnp.arange(half_rows, dtype=jnp.int32)
    )
    row_live = row_place < pick_entry(img_len, group_index)
    guided = jnp.where(row_live[:, None], guided, 0.0)
    start_rows = lax.dynamic_slice_in_dim(latents, cfg_index * half_rows, half_rows, 0)
    moved = start_rows - pick_entry(step_size, step_index) * guided
    return (guided[None], moved[None])


def solution(mesh):
    placed = (
        P(("group", "mp"), None),
        P("cfg", ("group", "mp"), None),
        P(),
        P(None, "mp"),
        P(None, "mp"),
        P(),
        P(),
        P(),
        P(),
        P(),
        P(),
        P(),
        P(),
        P(),
        P(),
        P(),
        P(),
        P(),
    )
    return jax.shard_map(
        local,
        mesh=mesh,
        in_specs=placed,
        out_specs=(P("cfg", ("group", "mp"), None), P("cfg", ("group", "mp"), None)),
        check_vma=False,
    )
```

profile of v0, /device:TPU:1, one launch (start us, length us, event | category | flops | bytes accessed | tf_op | source)
XLA Modules:
  0.0 342.4 jit_solution(17559711383967402021)
XLA Ops:
  7.2 1.3 dynamic_slice.51
  9.8 1.3 convert_reduce_fusion
  11.1 1.5 fusion.18
  13.3 1.0 dynamic-slice_add_fusion.1
  14.3 2.4 fusion.21
  16.8 1.5 fusion.50
  18.3 0.5 multiply_reduce_fusion.1
  18.8 1.6 constant_dynamic-slice_fusion
  20.3 1.8 add_convert_fusion.1
  22.5 0.7 fusion.48
  23.1 0.6 iota_compare_fusion.2
  23.8 0.6 iota_compare_fusion
  24.4 0.7 iota_compare_fusion.1
  25.1 34.8 %all-gather.3.cloned.1.call-done = bf16[512,3072]{1,0:T(8,128)(2,1)} async-done(((bf16[128,3072]{1,0:T(8,128)(2,1)}), bf16[512,3072]{1,0:T(8,128)(2,1)}) %all-gather.3.cloned.1.call-update) | async-done | bytes 3145744 | tf_op jit(solution)/shard_map/all_gather | solution.py:70
  59.9 7.0 %fusion.53 = f32[512,768]{1,0:T(8,128)} fusion(bf16[512,3072]{1,0:T(8,128)(2,1)} %all-gather.3.cloned.1.call-done, bf16[3072,768]{1,0:T(8,128)(2,1)} %param.22), kind=kOutput, calls=%fused_computation.97 | convolution fusion | flops 2415919104 | bytes 9437184 | tf_op jit(solution)/shard_map/dot_general | solution.py:78
  66.9 2.9 reshape.125
  69.8 2.1 slice.60
  72.5 55.0 %all-gather.5.cloned.1.call-done = bf16[1024,3072]{1,0:T(8,128)(2,1)} async-done(((bf16[256,3072]{1,0:T(8,128)(2,1)}), bf16[1024,3072]{1,0:T(8,128)(2,1)}) %all-gather.5.cloned.1.call-update) | async-done | bytes 6291472 | tf_op jit(solution)/shard_map/all_gather | solution.py:69
  127.5 11.3 %fusion.54 = f32[1024,1152]{0,1:T(8,128)S(1)} fusion(bf16[1024,3072]{1,0:T(8,128)(2,1)} %all-gather.5.cloned.1.call-done, bf16[3072,1152]{1,0:T(8,128)(2,1)} %param.21), kind=kOutput, calls=%fused_computation.98 | convolution fusion | flops 7247757312 | bytes 18087936 | tf_op jit(solution)/shard_map/dot_general | solution.py:72
  138.8 2.1 copy-done.2
  140.9 1.3 slice.61
  142.2 3.0 copy.40
  145.2 1.9 fusion.22
  147.1 1.9 fusion.24
  149.0 0.9 copy-done.4
  149.9 1.1 pad_maximum_fusion.2
  151.0 0.7 collective-permute-start.1
  151.7 0.6 iota_compare_fusion.3
  152.4 1.3 dynamic_slice.57
  154.3 0.6 pad_add_fusion
  154.9 3.1 slice.57
  158.0 2.9 copy.41
  160.9 1.5 fusion.30
  162.4 0.9 copy-done.3
  163.3 2.1 pad_maximum_fusion.1
  165.4 1.6 multiply_reduce_fusion.2
  167.0 19.6 %fusion.51 = (f32[3,1024]{1,0:T(4,128)}, f32[3,1024,3072]{2,1,0:T(8,128)}) fusion(pred[3072]{0:T(1024)(128)(4,1)} %pad_add_fusion, bf16[1536,3,128]{2,0,1:T(8,128)(2,1)} %collective-permute-done.1, bf16[1024,3,128]{2,0,1:T(8,128)(2,1)} %copy-done.4, bf16[512,3,128]{2,0,1:T(8,128)(2,1)S(1)} %multiply_convert_fusion.1, f32[1024,3,3,128]{0,3,2,1:T(8,128)} %bitcast.91, ...), kind=kOutput, calls=%fused_computation.95 | convolution fusion | flops 2461928448 | bytes 41709056 | tf_op jit(solution)/shard_map/sub | solution.py:102
  186.6 15.0 %fusion.26 = bf16[3,128,1024]{2,1,0:T(8,128)(2,1)S(1)} fusion(f32[3,1024,3072]{2,1,0:T(8,128)} %get-tuple-element.19, f32[3,1024]{1,0:T(4,128)} %get-tuple-element.18, bf16[1536,3,128]{0,2,1:T(8,128)(2,1)} %collective-permute-done, bf16[1024,3,128]{0,2,1:T(8,128)(2,1)} %copy-done.3, bf16[512,3,128]{0,2,1:T(8,128)(2,1)} %bitcast.93), kind=kOutput, calls=%fused_computation.42 | convolution fusion | flops 2442264576 | bytes 40906752 | tf_op jit(solution)/shard_map/hqk,khe->qhe/dot_general | solution.py:104
  201.7 8.1 %fusion.13 = f32[1024,3072]{1,0:T(8,128)} fusion(bf16[1024,384]{0,1:T(8,128)(2,1)S(1)} %bitcast.94, bf16[1536,3072]{1,0:T(8,128)(2,1)} %param.25, s32[]{:T(128)S(6)} %select_n.66), kind=kOutput, calls=%fused_computation.21 | convolution fusion | flops 2415919104 | bytes 15728644 | tf_op jit(solution)/shard_map/dot_general | solution.py:110
  209.8 1.4 dynamic-slice_add_fusion
  211.2 113.8 %reduce-scatter.2.cloned.1.call-done = f32[256,3072]{1,0:T(8,128)} async-done(((f32[1024,3072]{1,0:T(8,128)}), f32[256,3072]{1,0:T(8,128)}) %reduce-scatter.2.cloned.1.call-update) | async-done | bytes 3145744 | tf_op jit(solution)/shard_map/reduce_scatter | solution.py:109
  325.0 2.3 fusion.47
  328.4 0.8 fusion.52
  329.2 2.8 collective-permute-start.2
  332.0 0.7 add_compare_fusion
  332.7 0.7 dynamic_slice.63
  333.4 0.6 dynamic_slice.60
  334.0 1.9 subtract_bitcast_fusion
  (48 shorter events, 2.1 us)
Async XLA Ops:
  7.2 9.6 %copy-start = (bf16[64,3072]{1,0:T(8,128)(2,1)S(1)}, bf16[64,3072]{1,0:T(8,128)(2,1)}, u32[]{:S(2)}) copy-start(bf16[64,3072]{1,0:T(8,128)(2,1)} %param.20) | copy-start | bytes 1179652
  7.2 52.7 %all-gather.3.cloned.1.call-start = ((), (), s32[]{:S(2)}) async-start(), calls=%async_computation.1 | async-start | bytes 3932160 | tf_op jit(solution)/shard_map/all_gather | solution.py:70
  16.7 110.7 %all-gather.5.cloned.1.call-start = ((), (), s32[]{:S(2)}) async-start(), calls=%async_computation.2 | async-start | bytes 7864320 | tf_op jit(solution)/shard_map/all_gather | solution.py:69
  20.3 2.1 copy-start.8
  20.3 2.1 copy-start.9
  22.2 302.8 %reduce-scatter.2.cloned.1.call-start = ((), (), s32[]{:S(2)}) async-start(), calls=%async_computation.3 | async-start | bytes 15728640 | tf_op jit(solution)/shard_map/reduce_scatter | solution.py:109
  66.9 5.3 %copy-start.10 = (f32[128]{0:T(128)S(1)}, f32[128]{0:T(128)}, u32[]{:S(2)}) copy-start(f32[128]{0:T(128)} %param.24) | copy-start | bytes 1540
  138.8 2.2 copy-start.2
  149.0 0.9 copy-start.4
  151.0 16.0 %collective-permute-start.1 = (bf16[1536,3,128]{2,0,1:T(8,128)(2,1)}, bf16[1536,3,128]{2,0,1:T(8,128)(2,1)}, u32[]{:S(2)}, u32[]{:S(2)}) collective-permute-start(bf16[1536,3,128]{2,0,1:T(8,128)(2,1)} %pad_maximum_fusion.2), channel_id=1, source_target_pairs={{0,4},{4,0},{8,12},{12,8},{16,20},{20,16},{24,28},{28,24},{32,36},... | collective-permute-start | bytes 3538952 | tf_op jit(solution)/shard_map/ppermute | solution.py:12
  162.4 0.9 copy-start.3
  165.4 21.2 %collective-permute-start = (bf16[1536,3,128]{0,2,1:T(8,128)(2,1)}, bf16[1536,3,128]{0,2,1:T(8,128)(2,1)}, u32[]{:S(2)}, u32[]{:S(2)}) collective-permute-start(bf16[1536,3,128]{0,2,1:T(8,128)(2,1)} %pad_maximum_fusion.1), channel_id=1, source_target_pairs={{0,4},{4,0},{8,12},{12,8},{16,20},{20,16},{24,28},{28,24},{32,36},... | collective-permute-start | bytes 3538952 | tf_op jit(solution)/shard_map/ppermute | solution.py:12
  209.8 115.3 %copy-start.6 = (f32[1,1,3072]{2,0,1:T(1,128)S(1)}, f32[1,1,3072]{2,0,1:T(1,128)}, u32[]{:S(2)}) copy-start(f32[1,1,3072]{2,0,1:T(1,128)} %get-tuple-element.4) | copy-start | bytes 36868
  327.4 0.7 copy-start.7
  327.4 1.1 copy-start.11
  327.4 8.5 %copy-start.1 = (bf16[64,3072]{1,0:T(8,128)(2,1)S(1)}, bf16[64,3072]{1,0:T(8,128)(2,1)}, u32[]{:S(2)}) copy-start(bf16[64,3072]{1,0:T(8,128)(2,1)} %param.20) | copy-start | bytes 1179652
  327.4 5.3 %copy-start.12 = (f32[8]{0:T(128)S(1)}, f32[8]{0:T(128)}, u32[]{:S(2)}) copy-start(f32[8]{0:T(128)} %param.31) | copy-start | bytes 100
  327.4 6.0 %copy-start.13 = (f32[16]{0:T(128)S(1)}, f32[16]{0:T(128)}, u32[]{:S(2)}) copy-start(f32[16]{0:T(128)} %param.30) | copy-start | bytes 196
  327.4 6.6 %copy-start.5 = (f32[256,64]{0,1:T(8,128)S(1)}, f32[256,64]{0,1:T(8,128)}, u32[]{:S(2)}) copy-start(f32[256,64]{0,1:T(8,128)} %param.18) | copy-start | bytes 196612
  329.2 4.8 %collective-permute-start.2 = (bf16[256,64]{0,1:T(8,128)(2,1)S(1)}, bf16[256,64]{0,1:T(8,128)(2,1)S(1)}, u32[]{:S(2)}, u32[]{:S(2)}) collective-permute-start(bf16[256,64]{0,1:T(8,128)(2,1)S(1)} %get-tuple-element.20), channel_id=1, source_target_pairs={{0,64},{64,0},{1,65},{65,1},{2,66},{66,2},{3,67},{67,3},{4,68},{68... | collective-permute-start | bytes 98312 | tf_op jit(solution)/shard_map/ppermute | solution.py:12
Sparse Core Ops, SparseCore 0:
  16.8 42.9 all-gather.2
  61.5 65.8 all-gather.4
  209.9 115.0 reduce-scatter.1
where the time goes:
time: 343 us; the launch traced here: 342 us
  waiting for transfers between devices  204 us (59%)
  matrix products  63.3 us (18%)
  other arithmetic  27.7 us (8%)
  local copies, waits for them, and re-layouts  27.4 us (8%)
  between operations  16.7 us (5%)
  starting transfers between devices  3.83 us (1%)
    reduce_scatter x1, waiting for transfers between devices, local(): lax.psum_scatter(jnp.dot(mixed, w_local, preferred_element_type=jnp.float...  114 us
    all_gather x1, waiting for transfers between devices, local(): lax.all_gather(img_mod, 'mp', axis=0, tiled=True)  55 us
    all_gather x1, waiting for transfers between devices, local(): lax.all_gather(txt_mod, 'mp', axis=0, tiled=True)  34.8 us
    sub x1, matrix products, local(): weights = jnp.exp(scores - jnp.max(scores, -1, keepdims=True))  19.6 us
    dot_general x1, matrix products, local(): jnp.einsum('hqk,khe->qhe', probs, all_values, preferred_element_type=jnp....  15 us
    dot_general x1, matrix products, local(): jnp.dot(img_full, w_img_qkv, preferred_element_type=jnp.float32)  11.3 us
    unnamed x30, local copies, waits for them, and re-layouts  10.4 us
    dot_general x1, matrix products, local(): jnp.dot(mixed, w_local, preferred_element_type=jnp.float32)  8.09 us
  transfers between devices with their start and end apart: 6, of which 3 were waited for; matrix products, arithmetic and copies ran while one was open for 17% of the time, Pallas kernels for 0%

commit v1 on v0

--- a/solution.py
+++ b/solution.py
@@ -4,6 +4,15 @@
 from jax.sharding import PartitionSpec as P
 
 HD = 128
+cubes_write = lambda target: jnp.concatenate(
+    lax.all_to_all(
+        jnp.stack(lax.psum(1, axis_name="mp") * [target], axis=0),
+        axis_name="mp",
+        split_axis=0,
+        concat_axis=0,
+    ),
+    axis=0,
+)
 
 
 def partner(value, axis, bit):
@@ -65,10 +74,7 @@
     txt_mod = (
         layer_norm(text_hidden[0].astype(jnp.float32)) * (1.0 + text_rows[1]) + text_rows[0]
     ).astype(jnp.bfloat16)
-    img_full, txt_full = (
-        lax.all_gather(img_mod, "mp", axis=0, tiled=True),
-        lax.all_gather(txt_mod, "mp", axis=0, tiled=True),
-    )
+    img_full, txt_full = (lax.all_gather(img_mod, "mp", axis=0, tiled=True), cubes_write(txt_mod))
     qkv = jnp.dot(img_full, w_img_qkv, preferred_element_type=jnp.float32).reshape(
         full_img, local_heads, 3, HD
     )

time: 343 us -> 329 us (0.959)
  waiting for transfers between devices: 204 us -> 183 us
  starting transfers between devices: 3.83 us -> 9.21 us
    all_to_all x0 -> x1, waiting for transfers between devices: none -> 56.4 us  [lax.all_to_all(jnp.stack(lax.psum(1, axis_name='mp') * [target], axis=0),...]
    all_gather x1, waiting for transfers between devices: 55 us -> 13.7 us  [local(): lax.all_gather(img_mod, 'mp', axis=0, tiled=True)]
    all_gather x1 -> x0, waiting for transfers between devices: 34.8 us -> none  [local(): lax.all_gather(txt_mod, 'mp', axis=0, tiled=True)]
    dot_general x0 -> x1, local copies, waits for them, and re-layouts: none -> 7 us  [local(): jnp.dot(txt_full, w_txt_kv, preferred_element_type=jnp.float32)]
    all_to_all x0 -> x1, starting transfers between devices: none -> 5.85 us  [lax.all_to_all(jnp.stack(lax.psum(1, axis_name='mp') * [target], axis=0),...]
    slice x2 -> x0, local copies, waits for them, and re-layouts: 5.24 us -> none  [the longest x1 3.13 us: local(): value_txt = text_kv[:, :, 1].astype(jnp.bfloat16)]
    convert_element_type x0 -> x2, local copies, waits for them, and re-layouts: none -> 3.87 us  [local(): value_txt = text_kv[:, :, 1].astype(jnp.bfloat16)]
    unnamed x30 -> x33, local copies, waits for them, and re-layouts: 10.4 us -> 8.42 us
where the time goes in v1:
time: 329 us; the launch traced here: 327 us
  waiting for transfers between devices  183 us (56%)
  matrix products  62.6 us (19%)
  local copies, waits for them, and re-layouts  28.8 us (9%)
  other arithmetic  26.7 us (8%)
  between operations  17 us (5%)
  starting transfers between devices  9.21 us (3%)
    reduce_scatter x1, waiting for transfers between devices, local(): lax.psum_scatter(jnp.dot(mixed, w_local, preferred_element_type=jnp.float...  113 us
    all_to_all x1, waiting for transfers between devices, lax.all_to_all(jnp.stack(lax.psum(1, axis_name='mp') * [target], axis=0),...  56.4 us
    sub x1, matrix products, local(): weights = jnp.exp(scores - jnp.max(scores, -1, keepdims=True))  19.6 us
    dot_general x1, matrix products, local(): jnp.einsum('hqk,khe->qhe', probs, all_values, preferred_element_type=jnp....  15 us
    all_gather x1, waiting for transfers between devices, local(): lax.all_gather(img_mod, 'mp', axis=0, tiled=True)  13.7 us
    dot_general x1, matrix products, local(): jnp.dot(img_full, w_img_qkv, preferred_element_type=jnp.float32)  11.3 us
    unnamed x33, local copies, waits for them, and re-layouts  8.42 us
    dot_general x1, matrix products, local(): jnp.dot(mixed, w_local, preferred_element_type=jnp.float32)  8.09 us
  transfers between devices with their start and end apart: 6, of which 3 were waited for; matrix products, arithmetic and copies ran while one was open for 17% of the time, Pallas kernels for 0%

profile of v1, /device:TPU:1, one launch (start us, length us, event | category | flops | bytes accessed | tf_op | source)
XLA Modules:
  0.0 327.4 jit_solution(13361720315793575944)
XLA Ops:
  7.2 1.3 dynamic_slice.51
  9.8 1.5 fusion.52
  12.5 1.0 constant_dynamic-slice_fusion
  13.5 1.0 dynamic-slice_add_fusion.1
  14.4 1.9 add_convert_fusion.1
  16.3 1.3 convert_reduce_fusion
  17.6 1.5 fusion.21
  19.1 1.5 fusion.31
  20.7 2.0 stack.10
  22.7 5.8 %all-to-all-start = ((bf16[4,128,3072]{2,1,0:T(8,128)(2,1)}), bf16[4,128,3072]{2,1,0:T(8,128)(2,1)}, u32[]{:S(2)}, u32[]{:S(2)}) async-start(bf16[4,128,3072]{2,1,0:T(8,128)(2,1)} %stack.10), calls=%async_computation | async-start | bytes 6291456 | tf_op jit(solution)/shard_map/all_to_all | solution.py:8
  28.6 7.0 %copy.38 = bf16[768,3072]{1,0:T(8,128)(2,1)} copy(bf16[768,3072]{0,1:T(8,128)(2,1)} %bitcast.88) | data formatting | bytes 9437184 | tf_op jit(solution)/shard_map/dot_general | solution.py:84
  35.6 0.6 dynamic_slice.57
  36.8 0.7 fusion.50
  37.5 0.6 iota_compare_fusion.2
  38.1 0.7 iota_compare_fusion.3
  38.8 0.6 iota_compare_fusion
  39.4 0.7 iota_compare_fusion.1
  40.1 56.4 %all-to-all-done = bf16[4,128,3072]{2,1,0:T(8,128)(2,1)} async-done(((bf16[4,128,3072]{2,1,0:T(8,128)(2,1)}), bf16[4,128,3072]{2,1,0:T(8,128)(2,1)}, u32[]{:S(2)}, u32[]{:S(2)}) %all-to-all-start) | async-done | bytes 3145760 | tf_op jit(solution)/shard_map/all_to_all | solution.py:8
  96.5 6.3 %fusion.55 = f32[512,3,2,128]{3,0,2,1:T(8,128)S(1)} fusion(bf16[512,3072,1,1]{1,0,3,2:T(8,128)(2,1)} %bitcast.9, bf16[3,2,128,3072]{3,2,1,0:T(8,128)(2,1)} %bitcast.89), kind=kOutput, calls=%fused_computation.100 | convolution fusion | flops 2415919104 | bytes 9437184 | tf_op jit(solution)/shard_map/dot_general | solution.py:84
  103.1 0.8 copy-done.5
  104.2 13.7 %all-gather.2.cloned.1.call-done = bf16[1024,3072]{1,0:T(8,128)(2,1)} async-done(((bf16[256,3072]{1,0:T(8,128)(2,1)}), bf16[1024,3072]{1,0:T(8,128)(2,1)}) %all-gather.2.cloned.1.call-update) | async-done | bytes 6291472 | tf_op jit(solution)/shard_map/all_gather | solution.py:77
  117.9 11.3 %fusion.56 = f32[1024,1152]{0,1:T(8,128)S(1)} fusion(bf16[1024,3072]{1,0:T(8,128)(2,1)} %all-gather.2.cloned.1.call-done, bf16[3072,1152]{1,0:T(8,128)(2,1)} %param.21), kind=kOutput, calls=%fused_computation.101 | convolution fusion | flops 7247757312 | bytes 18087936 | tf_op jit(solution)/shard_map/dot_general | solution.py:78
  129.2 2.1 copy-done.2
  131.3 1.3 slice.61
  132.6 3.0 copy.43
  135.6 1.9 fusion.22
  137.5 1.9 fusion.24
  139.4 0.9 copy-done.4
  140.4 1.1 pad_maximum_fusion.2
  141.9 1.9 fusion.32
  143.8 1.9 copy.32
  145.8 1.5 fusion.30
  147.3 0.9 copy-done.3
  148.2 2.1 pad_maximum_fusion.1
  150.4 1.6 multiply_reduce_fusion.2
  151.9 0.6 add_rsqrt_fusion.1
  152.6 19.6 %fusion.53 = (f32[3,1024]{1,0:T(4,128)}, f32[3,1024,3072]{2,1,0:T(8,128)}) fusion(pred[3072]{0:T(1024)(128)(4,1)S(1)} %pad_add_fusion, bf16[1536,3,128]{2,0,1:T(8,128)(2,1)} %collective-permute-done.1, bf16[1024,3,128]{2,0,1:T(8,128)(2,1)} %copy-done.4, bf16[512,3,128]{2,0,1:T(8,128)(2,1)S(1)} %multiply_convert_fusion.1, f32[1024,3,3,128]{0,3,2,1:T(8,128)} %bitcast.93, ...), kind=kOutput, calls=%fused_computation.98 | convolution fusion | flops 2461928448 | bytes 41713152 | tf_op jit(solution)/shard_map/sub | solution.py:108
  172.2 15.0 %fusion.26 = bf16[3,128,1024]{2,1,0:T(8,128)(2,1)S(1)} fusion(f32[3,1024,3072]{2,1,0:T(8,128)} %get-tuple-element.19, f32[3,1024]{1,0:T(4,128)} %get-tuple-element.18, bf16[1536,3,128]{0,2,1:T(8,128)(2,1)} %collective-permute-done, bf16[1024,3,128]{0,2,1:T(8,128)(2,1)} %copy-done.3, bf16[512,3,128]{0,2,1:T(8,128)(2,1)} %copy.32), kind=kOutput, calls=%fused_computation.43 | convolution fusion | flops 2442264576 | bytes 40906752 | tf_op jit(solution)/shard_map/hqk,khe->qhe/dot_general | solution.py:110
  187.2 8.1 %fusion.13 = f32[1024,3072]{1,0:T(8,128)} fusion(bf16[1024,384]{0,1:T(8,128)(2,1)S(1)} %bitcast.94, bf16[1536,3072]{1,0:T(8,128)(2,1)} %param.25, s32[]{:T(128)S(6)} %select_n.66), kind=kOutput, calls=%fused_computation.24 | convolution fusion | flops 2415919104 | bytes 15728644 | tf_op jit(solution)/shard_map/dot_general | solution.py:116
  195.3 1.4 dynamic-slice_add_fusion
  196.8 113.1 %reduce-scatter.2.cloned.1.call-done = f32[256,3072]{1,0:T(8,128)} async-done(((f32[1024,3072]{1,0:T(8,128)}), f32[256,3072]{1,0:T(8,128)}) %reduce-scatter.2.cloned.1.call-update) | async-done | bytes 3145744 | tf_op jit(solution)/shard_map/reduce_scatter | solution.py:115
  309.9 2.3 fusion.49
  313.3 0.8 fusion.54
  314.0 2.8 collective-permute-start.2
  316.9 0.7 add_compare_fusion
  317.6 0.6 dynamic_slice.63
  318.2 0.6 dynamic_slice.60
  318.8 1.8 subtract_bitcast_fusion
  (51 shorter events, 2.8 us)
Async XLA Ops:
  7.2 2.6 copy-start
  7.2 110.7 %all-gather.2.cloned.1.call-start = ((), (), s32[]{:S(2)}) async-start(), calls=%async_computation.2 | async-start | bytes 7864320 | tf_op jit(solution)/shard_map/all_gather | solution.py:77
  22.7 73.8 %all-to-all-start = ((bf16[4,128,3072]{2,1,0:T(8,128)(2,1)}), bf16[4,128,3072]{2,1,0:T(8,128)(2,1)}, u32[]{:S(2)}, u32[]{:S(2)}) async-start(bf16[4,128,3072]{2,1,0:T(8,128)(2,1)} %stack.10), calls=%async_computation | async-start | bytes 6291456 | tf_op jit(solution)/shard_map/all_to_all | solution.py:8
  28.5 281.3 %reduce-scatter.2.cloned.1.call-start = ((), (), s32[]{:S(2)}) async-start(), calls=%async_computation.3 | async-start | bytes 15728640 | tf_op jit(solution)/shard_map/reduce_scatter | solution.py:115
  28.5 7.0 %copy-start.12 = (s32[2,16]{1,0:T(2,128)S(1)}, s32[2,16]{1,0:T(2,128)}, u32[]{:S(2)}) copy-start(s32[2,16]{1,0:T(2,128)} %param.34) | copy-start | bytes 388
  28.5 8.3 %copy-start.9 = (s32[16]{0:T(128)S(1)}, s32[16]{0:T(128)}, u32[]{:S(2)}) copy-start(s32[16]{0:T(128)} %param.33) | copy-start | bytes 196
  28.5 8.3 %copy-start.10 = (s32[16]{0:T(128)S(1)}, s32[16]{0:T(128)}, u32[]{:S(2)}) copy-start(s32[16]{0:T(128)} %param.32) | copy-start | bytes 196
  96.5 7.4 %copy-start.11 = (f32[128]{0:T(128)S(1)}, f32[128]{0:T(128)}, u32[]{:S(2)}) copy-start(f32[128]{0:T(128)} %param.24) | copy-start | bytes 1540
  102.8 1.1 copy-start.5
  129.2 2.1 copy-start.2
  139.4 0.9 copy-start.4
  141.4 11.1 %collective-permute-start.1 = (bf16[1536,3,128]{2,0,1:T(8,128)(2,1)}, bf16[1536,3,128]{2,0,1:T(8,128)(2,1)}, u32[]{:S(2)}, u32[]{:S(2)}) collective-permute-start(bf16[1536,3,128]{2,0,1:T(8,128)(2,1)} %pad_maximum_fusion.2), channel_id=1, source_target_pairs={{0,4},{4,0},{8,12},{12,8},{16,20},{20,16},{24,28},{28,24},{32,36},... | collective-permute-start | bytes 3538952 | tf_op jit(solution)/shard_map/ppermute | solution.py:21
  147.3 0.9 copy-start.3
  150.3 21.9 %collective-permute-start = (bf16[1536,3,128]{0,2,1:T(8,128)(2,1)}, bf16[1536,3,128]{0,2,1:T(8,128)(2,1)}, u32[]{:S(2)}, u32[]{:S(2)}) collective-permute-start(bf16[1536,3,128]{0,2,1:T(8,128)(2,1)} %pad_maximum_fusion.1), channel_id=1, source_target_pairs={{0,4},{4,0},{8,12},{12,8},{16,20},{20,16},{24,28},{28,24},{32,36},... | collective-permute-start | bytes 3538952 | tf_op jit(solution)/shard_map/ppermute | solution.py:21
  312.2 0.7 copy-start.7
  312.2 0.7 copy-start.8
  312.2 1.1 copy-start.13
  312.2 8.4 %copy-start.1 = (bf16[64,3072]{1,0:T(8,128)(2,1)S(1)}, bf16[64,3072]{1,0:T(8,128)(2,1)}, u32[]{:S(2)}) copy-start(bf16[64,3072]{1,0:T(8,128)(2,1)} %param.20) | copy-start | bytes 1179652
  312.2 5.3 %copy-start.14 = (f32[8]{0:T(128)S(1)}, f32[8]{0:T(128)}, u32[]{:S(2)}) copy-start(f32[8]{0:T(128)} %param.31) | copy-start | bytes 100
  312.3 5.9 %copy-start.15 = (f32[16]{0:T(128)S(1)}, f32[16]{0:T(128)}, u32[]{:S(2)}) copy-start(f32[16]{0:T(128)} %param.30) | copy-start | bytes 196
  312.3 6.5 %copy-start.6 = (f32[256,64]{0,1:T(8,128)S(1)}, f32[256,64]{0,1:T(8,128)}, u32[]{:S(2)}) copy-start(f32[256,64]{0,1:T(8,128)} %param.18) | copy-start | bytes 196612
  314.0 4.7 %collective-permute-start.2 = (bf16[256,64]{0,1:T(8,128)(2,1)S(1)}, bf16[256,64]{0,1:T(8,128)(2,1)S(1)}, u32[]{:S(2)}, u32[]{:S(2)}) collective-permute-start(bf16[256,64]{0,1:T(8,128)(2,1)S(1)} %get-tuple-element.20), channel_id=1, source_target_pairs={{0,64},{64,0},{1,65},{65,1},{2,66},{66,2},{3,67},{67,3},{4,68},{68... | collective-permute-start | bytes 98312 | tf_op jit(solution)/shard_map/ppermute | solution.py:21
Sparse Core Ops, SparseCore 0:
  16.4 101.4 all-gather.1
  195.4 114.3 reduce-scatter.1
